TPU v7x, 32 devices: a whole 2x2x4 slice. The times are simulated.
32 devices in a mesh: dp: 4 (over y, x), fsdp: 8 (over z, core).
Axes of the slice: x: 2, y: 2, z: 4, core: 2. Of those that a mesh axis runs over, the one named last changes fastest.
Arguments:
- layer_input: bfloat16 [64, 256, 768], P(('dp', 'fsdp')), may hold values from -6 to 6
- encoder_states: bfloat16 [64, 256, 768], P(('dp', 'fsdp')), may hold values from -6 to 6
- output_grad: bfloat16 [64, 256, 768], P(('dp', 'fsdp')), may hold values from -6 to 6
- span_start: int32 [64], P(('dp', 'fsdp')), may hold values from 0 to 128, as said below
- span_length: int32 [64], P(('dp', 'fsdp')), may hold values from 128 to 256, as said below
- self_project: bfloat16 [3, 768, 768], P(None, ('dp', 'fsdp')), may hold values from -0.21875 to 0.21875
- self_output: bfloat16 [768, 768], P(('dp', 'fsdp')), may hold values from -1.75 to 1.75
- cross_project: bfloat16 [3, 768, 768], P(None, ('dp', 'fsdp')), may hold values from -0.21875 to 0.21875
- cross_output: bfloat16 [768, 768], P(('dp', 'fsdp')), may hold values from -1.75 to 1.75
- attend_bias: bfloat16 [6, 768], P(None, ('dp', 'fsdp')), may hold values from -1.796875 to 1.796875
- expand_weight: bfloat16 [768, 3072], P(('dp', 'fsdp')), may hold values from -0.21875 to 0.21875
- expand_bias: bfloat16 [3072], P(('dp', 'fsdp')), may hold values from -1.796875 to 1.796875
- contract_weight: bfloat16 [3072, 768], P(('dp', 'fsdp')), may hold values from -0.109375 to 0.109375
- contract_bias: bfloat16 [768], P(('dp', 'fsdp')), may hold values from -1.796875 to 1.796875
- norm_gain: bfloat16 [3, 768], P(None, ('dp', 'fsdp')), may hold values from 0.25 to 1.75
- norm_shift: bfloat16 [3, 768], P(None, ('dp', 'fsdp')), may hold values from -1.796875 to 1.796875
Outputs:
- layer_output: bfloat16 [64, 256, 768], P(('dp', 'fsdp'))
- input_grad: float32 [64, 256, 768], P(('dp', 'fsdp'))
- encoder_grad: float32 [64, 256, 768], P(('dp', 'fsdp'))
- self_project_grad: float32 [3, 768, 768], P(None, ('dp', 'fsdp'))
- self_output_grad: float32 [768, 768], P(('dp', 'fsdp'))
- cross_project_grad: float32 [3, 768, 768], P(None, ('dp', 'fsdp'))
- cross_output_grad: float32 [768, 768], P(('dp', 'fsdp'))
- attend_bias_grad: float32 [6, 768], P(None, ('dp', 'fsdp'))
- expand_weight_grad: float32 [768, 3072], P(('dp', 'fsdp'))
- expand_bias_grad: float32 [3072], P(('dp', 'fsdp'))
- contract_weight_grad: float32 [3072, 768], P(('dp', 'fsdp'))
- contract_bias_grad: float32 [768], P(('dp', 'fsdp'))
- norm_gain_grad: float32 [3, 768], P(None, ('dp', 'fsdp'))
- norm_shift_grad: float32 [3, 768], P(None, ('dp', 'fsdp'))
Inputs may be any that keep to these rules, and one draw needn't show every extreme that they name: span_start + span_length <= 256 for every sequence; some sequence has its span start at 0, some at 128. `span_length`: some sequence has a span of exactly 256 tokens and some of exactly 128.
All inputs are finite; a program needn't handle non-finite values.
Results may differ from a plain program's by a relative error of at most 0.025.
Values may be sent and summed in bfloat16 or wider, within the bound.
No kernel may reach another device: no remote copies, remote signals or barrier semaphores. Data moves between devices by JAX's collectives and lax.ppermute only.
A program may use at most 256 MiB of HBM per device.

v0:
```python
import jax
import jax.numpy as jnp
from jax import lax
from jax.sharding import PartitionSpec as P

D = 768
H = 12
HD = 64
FF = 3072


eps_norm = 1e-05
big_negative = -1000000000.0
owner_dims = (1, 0, 1, 0, 1, 0, 0, 0, 0, 1, 1)


def layer_norm(summed, gain, shift):
    centre = summed - jnp.mean(summed, axis=-1, keepdims=True)
    spread = jnp.mean(centre * centre, axis=-1, keepdims=True)
    return centre * lax.rsqrt(spread + eps_norm) * gain + shift


def gelu_exact(value):
    return jax.nn.gelu(value, approximate=False)


def project(left_side, right_side):
    return jnp.dot(left_side, right_side, preferred_element_type=jnp.float32)


def project_left(left_side, right_side):
    return lax.dot_general(
        left_side, right_side, (((0,), (0,)), ((), ())), preferred_element_type=jnp.float32
    )


def project_back(grad_rows, weight):
    return lax.dot_general(
        grad_rows, weight, (((1,), (1,)), ((), ())), preferred_element_type=jnp.float32
    )


def split_heads(tensor):
    return tensor.reshape(tensor.shape[0], H, HD)


def norm_pullback(summed, gain, shift, grad_out):
    unused, pullback = jax.vjp(layer_norm, summed, gain, shift)
    return pullback(grad_out)


def span_mask(start, length, count):
    places = lax.iota(jnp.int32, count)
    inside = (places >= start) & (places < start + length)
    return (places[None, :] <= places[:, None]) | inside[:, None] & inside[None, :]


def score_block(queries, key_rows, allowed):
    scores = jnp.einsum(
        "qhe,khe->hqk",
        split_heads(queries),
        split_heads(key_rows),
        preferred_element_type=jnp.float32,
    )
    if allowed is None:
        return scores
    return jnp.where(allowed[None], scores, big_negative)


def attend_forward(queries, key_rows, values, allowed):
    scores = score_block(queries, key_rows, allowed)
    peak_score = jnp.max(scores, axis=2, keepdims=True)
    exp_scores = jnp.exp(scores - peak_score)
    exp_total = jnp.sum(exp_scores, axis=2, keepdims=True)
    soft_weights = (exp_scores / exp_total).astype(jnp.bfloat16)
    attended = jnp.einsum(
        "hqk,khe->qhe", soft_weights, split_heads(values), preferred_element_type=jnp.float32
    )
    return (
        attended.reshape(queries.shape[0], D).astype(jnp.bfloat16),
        peak_score + jnp.log(exp_total),
    )


def attend_backward(queries, key_rows, values, allowed, log_total, grad_mixed):
    scores = score_block(queries, key_rows, allowed)
    soft_weights = jnp.exp(scores - log_total)
    grad_heads = split_heads(grad_mixed)
    grad_soft = jnp.einsum(
        "qhe,khe->hqk", grad_heads, split_heads(values), preferred_element_type=jnp.float32
    )
    centre = jnp.sum(soft_weights * grad_soft, axis=2, keepdims=True)
    grad_scores = (soft_weights * (grad_soft - centre)).astype(jnp.bfloat16)
    row_count = queries.shape[0]
    key_count = key_rows.shape[0]
    grad_query = jnp.einsum(
        "hqk,khe->qhe", grad_scores, split_heads(key_rows), preferred_element_type=jnp.float32
    )
    grad_key = jnp.einsum(
        "hqk,qhe->khe", grad_scores, split_heads(queries), preferred_element_type=jnp.float32
    )
    grad_value = jnp.einsum(
        "hqk,qhe->khe",
        soft_weights.astype(jnp.bfloat16),
        grad_heads,
        preferred_element_type=jnp.float32,
    )
    return (
        grad_query.reshape(row_count, D).astype(jnp.bfloat16),
        grad_key.reshape(key_count, D).astype(jnp.bfloat16),
        grad_value.reshape(key_count, D).astype(jnp.bfloat16),
    )


def forward_one(tokens, memory, allowed, weights):
    (
        self_project,
        self_output,
        cross_project,
        cross_output,
        attend_bias,
        expand_weight,
        expand_bias,
        contract_weight,
        contract_bias,
        norm_gain,
        norm_shift,
    ) = weights
    biases = attend_bias.astype(jnp.float32)
    gain_rows = norm_gain.astype(jnp.float32)
    shift_rows = norm_shift.astype(jnp.float32)
    queries = ((project(tokens, self_project[0]) + biases[0]) * 0.125).astype(jnp.bfloat16)
    key_rows = project(tokens, self_project[1]).astype(jnp.bfloat16)
    values = (project(tokens, self_project[2]) + biases[1]).astype(jnp.bfloat16)
    attended, self_lse = attend_forward(queries, key_rows, values, allowed)
    first_sum = tokens.astype(jnp.float32) + (project(attended, self_output) + biases[2])
    first_norm = layer_norm(first_sum, gain_rows[0], shift_rows[0])
    first_low = first_norm.astype(jnp.bfloat16)
    cross_queries = ((project(first_low, cross_project[0]) + biases[3]) * 0.125).astype(
        jnp.bfloat16
    )
    cross_keys = project(memory, cross_project[1]).astype(jnp.bfloat16)
    cross_values = (project(memory, cross_project[2]) + biases[4]).astype(jnp.bfloat16)
    cross_mixed, cross_lse = attend_forward(cross_queries, cross_keys, cross_values, None)
    second_sum = first_norm + (project(cross_mixed, cross_output) + biases[5])
    second_norm = layer_norm(second_sum, gain_rows[1], shift_rows[1])
    second_low = second_norm.astype(jnp.bfloat16)
    hidden_pre = project(second_low, expand_weight) + expand_bias.astype(jnp.float32)
    hidden_act = gelu_exact(hidden_pre).astype(jnp.bfloat16)
    third_sum = second_norm + (
        project(hidden_act, contract_weight) + contract_bias.astype(jnp.float32)
    )
    output = layer_norm(third_sum, gain_rows[2], shift_rows[2])
    saved = (
        queries,
        key_rows,
        values,
        attended,
        self_lse,
        first_sum,
        first_low,
        cross_queries,
        cross_keys,
        cross_values,
        cross_mixed,
        cross_lse,
        second_sum,
        second_low,
        hidden_pre,
        hidden_act,
        third_sum,
    )
    return (output, saved)


def backward_one(tokens, memory, allowed, weights, saved, grad_output):
    (
        self_project,
        self_output,
        cross_project,
        cross_output,
        attend_bias,
        expand_weight,
        expand_bias,
        contract_weight,
        contract_bias,
        norm_gain,
        norm_shift,
    ) = weights
    (
        queries,
        key_rows,
        values,
        attended,
        self_lse,
        first_sum,
        first_low,
        cross_queries,
        cross_keys,
        cross_values,
        cross_mixed,
        cross_lse,
        second_sum,
        second_low,
        hidden_pre,
        hidden_act,
        third_sum,
    ) = saved
    gain_rows = norm_gain.astype(jnp.float32)
    shift_rows = norm_shift.astype(jnp.float32)
    grad_third, gain_last, shift_last = norm_pullback(
        third_sum, gain_rows[2], shift_rows[2], grad_output
    )
    grad_branch = grad_third.astype(jnp.bfloat16)
    contract_grad = project_left(hidden_act, grad_branch)
    contract_bias_grad = jnp.sum(grad_branch, axis=0, dtype=jnp.float32)
    grad_act = project_back(grad_branch, contract_weight)
    unused, gelu_pull = jax.vjp(gelu_exact, hidden_pre)
    grad_hidden = gelu_pull(grad_act)[0].astype(jnp.bfloat16)
    expand_grad = project_left(second_low, grad_hidden)
    expand_bias_grad = jnp.sum(grad_hidden, axis=0, dtype=jnp.float32)
    grad_second = grad_third + project_back(grad_hidden, expand_weight)
    grad_second_sum, gain_middle, shift_middle = norm_pullback(
        second_sum, gain_rows[1], shift_rows[1], grad_second
    )
    grad_cross = grad_second_sum.astype(jnp.bfloat16)
    cross_output_grad = project_left(cross_mixed, grad_cross)
    grad_cross_mixed = project_back(grad_cross, cross_output).astype(jnp.bfloat16)
    grad_cross_query, grad_cross_key, grad_cross_value = attend_backward(
        cross_queries, cross_keys, cross_values, None, cross_lse, grad_cross_mixed
    )
    cross_query_scaled = grad_cross_query * 0.125
    cross_grads = jnp.stack(
        [
            project_left(first_low, cross_query_scaled),
            project_left(memory, grad_cross_key),
            project_left(memory, grad_cross_value),
        ]
    )
    encoder_grad = project_back(grad_cross_key, cross_project[1]) + project_back(
        grad_cross_value, cross_project[2]
    )
    grad_first = grad_second_sum + project_back(cross_query_scaled, cross_project[0])
    grad_first_sum, gain_first, shift_first = norm_pullback(
        first_sum, gain_rows[0], shift_rows[0], grad_first
    )
    grad_self = grad_first_sum.astype(jnp.bfloat16)
    self_output_grad = project_left(attended, grad_self)
    grad_attended = project_back(grad_self, self_output).astype(jnp.bfloat16)
    grad_self_query, grad_self_key, grad_self_value = attend_backward(
        queries, key_rows, values, allowed, self_lse, grad_attended
    )
    self_query_scaled = grad_self_query * 0.125
    self_grads = jnp.stack(
        [
            project_left(tokens, self_query_scaled),
            project_left(tokens, grad_self_key),
            project_left(tokens, grad_self_value),
        ]
    )
    input_grad = (
        grad_first_sum
        + project_back(self_query_scaled, self_project[0])
        + project_back(grad_self_key, self_project[1])
        + project_back(grad_self_value, self_project[2])
    )
    bias_grads = jnp.stack(
        [
            jnp.sum(self_query_scaled, axis=0, dtype=jnp.float32),
            jnp.sum(grad_self_value, axis=0, dtype=jnp.float32),
            jnp.sum(grad_self, axis=0, dtype=jnp.float32),
            jnp.sum(cross_query_scaled, axis=0, dtype=jnp.float32),
            jnp.sum(grad_cross_value, axis=0, dtype=jnp.float32),
            jnp.sum(grad_cross, axis=0, dtype=jnp.float32),
        ]
    )
    grads = (
        self_grads,
        self_output_grad,
        cross_grads,
        cross_output_grad,
        bias_grads,
        expand_grad,
        expand_bias_grad,
        contract_grad,
        contract_bias_grad,
        jnp.stack([gain_first, gain_middle, gain_last]),
        jnp.stack([shift_first, shift_middle, shift_last]),
    )
    return (grads, input_grad, encoder_grad)


def gather_weights(shards):
    (
        self_project,
        self_output,
        cross_project,
        cross_output,
        attend_bias,
        expand_weight,
        expand_bias,
        contract_weight,
        contract_bias,
        norm_gain,
        norm_shift,
    ) = shards
    return (
        lax.all_gather(self_project, ("dp", "fsdp"), axis=1, tiled=True),
        lax.all_gather(self_output, ("dp", "fsdp"), axis=0, tiled=True),
        lax.all_gather(cross_project, ("dp", "fsdp"), axis=1, tiled=True),
        lax.all_gather(cross_output, ("dp", "fsdp"), axis=0, tiled=True),
        lax.all_gather(attend_bias, ("dp", "fsdp"), axis=1, tiled=True),
        lax.all_gather(expand_weight, ("dp", "fsdp"), axis=0, tiled=True),
        lax.all_gather(expand_bias, ("dp", "fsdp"), axis=0, tiled=True),
        lax.all_gather(contract_weight, ("dp", "fsdp"), axis=0, tiled=True),
        lax.all_gather(contract_bias, ("dp", "fsdp"), axis=0, tiled=True),
        lax.all_gather(norm_gain, ("dp", "fsdp"), axis=1, tiled=True),
        lax.all_gather(norm_shift, ("dp", "fsdp"), axis=1, tiled=True),
    )


def reduce_grads(totals):
    outer_count = lax.axis_size("dp")
    inner_count = lax.axis_size("fsdp")
    packed = []
    fronts = []
    for gradient, owner in zip(totals, owner_dims):
        front = jnp.moveaxis(gradient, owner, 0)
        fronts.append(front.shape)
        packed.append(front.reshape(1, outer_count, inner_count, -1))
    received = (
        lax.all_to_all(
            packed[0].astype(jnp.bfloat16), "fsdp", split_axis=2, concat_axis=0, tiled=True
        ).astype(jnp.float32),
        lax.all_to_all(
            packed[1].astype(jnp.bfloat16), "fsdp", split_axis=2, concat_axis=0, tiled=True
        ).astype(jnp.float32),
        lax.all_to_all(
            packed[2].astype(jnp.bfloat16), "fsdp", split_axis=2, concat_axis=0, tiled=True
        ).astype(jnp.float32),
        lax.all_to_all(
            packed[3].astype(jnp.bfloat16), "fsdp", split_axis=2, concat_axis=0, tiled=True
        ).astype(jnp.float32),
        lax.all_to_all(
            packed[4].astype(jnp.bfloat16), "fsdp", split_axis=2, concat_axis=0, tiled=True
        ).astype(jnp.float32),
        lax.all_to_all(
            packed[5].astype(jnp.bfloat16), "fsdp", split_axis=2, concat_axis=0, tiled=True
        ).astype(jnp.float32),
        lax.all_to_all(
            packed[6].astype(jnp.bfloat16), "fsdp", split_axis=2, concat_axis=0, tiled=True
        ).astype(jnp.float32),
        lax.all_to_all(
            packed[7].astype(jnp.bfloat16), "fsdp", split_axis=2, concat_axis=0, tiled=True
        ).astype(jnp.float32),
        lax.all_to_all(
            packed[8].astype(jnp.bfloat16), "fsdp", split_axis=2, concat_axis=0, tiled=True
        ).astype(jnp.float32),
        lax.all_to_all(
            packed[9].astype(jnp.bfloat16), "fsdp", split_axis=2, concat_axis=0, tiled=True
        ).astype(jnp.float32),
        lax.all_to_all(
            packed[10].astype(jnp.bfloat16), "fsdp", split_axis=2, concat_axis=0, tiled=True
        ).astype(jnp.float32),
    )
    partial_value = []
    for pieces, shape, owner in zip(received, fronts, owner_dims):
        summed = jnp.sum(pieces, axis=0)
        block_rows = shape[0] // (outer_count * inner_count)
        rows = summed.reshape((outer_count * block_rows,) + shape[1:])
        partial_value.append(jnp.moveaxis(rows, 0, owner))
    return (
        lax.psum_scatter(
            partial_value[0].astype(jnp.bfloat16), "dp", scatter_dimension=1, tiled=True
        ).astype(jnp.float32),
        lax.psum_scatter(
            partial_value[1].astype(jnp.bfloat16), "dp", scatter_dimension=0, tiled=True
        ).astype(jnp.float32),
        lax.psum_scatter(
            partial_value[2].astype(jnp.bfloat16), "dp", scatter_dimension=1, tiled=True
        ).astype(jnp.float32),
        lax.psum_scatter(
            partial_value[3].astype(jnp.bfloat16), "dp", scatter_dimension=0, tiled=True
        ).astype(jnp.float32),
        lax.psum_scatter(
            partial_value[4].astype(jnp.bfloat16), "dp", scatter_dimension=1, tiled=True
        ).astype(jnp.float32),
        lax.psum_scatter(
            partial_value[5].astype(jnp.bfloat16), "dp", scatter_dimension=0, tiled=True
        ).astype(jnp.float32),
        lax.psum_scatter(
            partial_value[6].astype(jnp.bfloat16), "dp", scatter_dimension=0, tiled=True
        ).astype(jnp.float32),
        lax.psum_scatter(
            partial_value[7].astype(jnp.bfloat16), "dp", scatter_dimension=0, tiled=True
        ).astype(jnp.float32),
        lax.psum_scatter(
            partial_value[8].astype(jnp.bfloat16), "dp", scatter_dimension=0, tiled=True
        ).astype(jnp.float32),
        lax.psum_scatter(
            partial_value[9].astype(jnp.bfloat16), "dp", scatter_dimension=1, tiled=True
        ).astype(jnp.float32),
        lax.psum_scatter(
            partial_value[10].astype(jnp.bfloat16), "dp", scatter_dimension=1, tiled=True
        ).astype(jnp.float32),
    )


def empty_grads():
    return (
        jnp.zeros((3, D, D), jnp.float32),
        jnp.zeros((D, D), jnp.float32),
        jnp.zeros((3, D, D), jnp.float32),
        jnp.zeros((D, D), jnp.float32),
        jnp.zeros((6, D), jnp.float32),
        jnp.zeros((D, FF), jnp.float32),
        jnp.zeros((FF,), jnp.float32),
        jnp.zeros((FF, D), jnp.float32),
        jnp.zeros((D,), jnp.float32),
        jnp.zeros((3, D), jnp.float32),
        jnp.zeros((3, D), jnp.float32),
    )


def body(
    layer_input,
    encoder_states,
    output_grad,
    span_start,
    span_length,
    self_project,
    self_output,
    cross_project,
    cross_output,
    attend_bias,
    expand_weight,
    expand_bias,
    contract_weight,
    contract_bias,
    norm_gain,
    norm_shift,
):
    shards = (
        self_project,
        self_output,
        cross_project,
        cross_output,
        attend_bias,
        expand_weight,
        expand_bias,
        contract_weight,
        contract_bias,
        norm_gain,
        norm_shift,
    )
    entries = (layer_input, encoder_states, output_grad, span_start, span_length)
    seq_tokens = layer_input.shape[1]

    def forward_step(carried, entry):
        tokens, memory, grad_rows, start, length = entry
        weights = gather_weights(shards)
        output, unused = forward_one(tokens, memory, span_mask(start, length, seq_tokens), weights)
        return (carried, output.astype(jnp.bfloat16))

    unused_carry, outputs = lax.scan(forward_step, jnp.zeros((), jnp.float32), entries)

    def backward_step(totals, entry):
        tokens, memory, grad_rows, start, length = entry
        weights = gather_weights(shards)
        allowed = span_mask(start, length, seq_tokens)
        unused, saved = forward_one(tokens, memory, allowed, weights)
        grads, input_grad, encoder_grad = backward_one(
            tokens, memory, allowed, weights, saved, grad_rows.astype(jnp.float32)
        )
        return (jax.tree.map(jnp.add, totals, grads), (input_grad, encoder_grad))

    totals, (input_grads, encoder_grads) = lax.scan(backward_step, empty_grads(), entries)
    owned = reduce_grads(totals)
    return (
        outputs,
        input_grads,
        encoder_grads,
        owned[0],
        owned[1],
        owned[2],
        owned[3],
        owned[4],
        owned[5],
        owned[6],
        owned[7],
        owned[8],
        owned[9],
        owned[10],
    )


def solution(mesh):
    return jax.shard_map(
        body,
        mesh=mesh,
        in_specs=(
            P(("dp", "fsdp"), None, None),
            P(("dp", "fsdp"), None, None),
            P(("dp", "fsdp"), None, None),
            P(("dp", "fsdp")),
            P(("dp", "fsdp")),
            P(None, ("dp", "fsdp"), None),
            P(("dp", "fsdp"), None),
            P(None, ("dp", "fsdp"), None),
            P(("dp", "fsdp"), None),
            P(None, ("dp", "fsdp")),
            P(("dp", "fsdp"), None),
            P(("dp", "fsdp")),
            P(("dp", "fsdp"), None),
            P(("dp", "fsdp")),
            P(None, ("dp", "fsdp")),
            P(None, ("dp", "fsdp")),
        ),
        out_specs=(
            P(("dp", "fsdp"), None, None),
            P(("dp", "fsdp"), None, None),
            P(("dp", "fsdp"), None, None),
            P(None, ("dp", "fsdp"), None),
            P(("dp", "fsdp"), None),
            P(None, ("dp", "fsdp"), None),
            P(("dp", "fsdp"), None),
            P(None, ("dp", "fsdp")),
            P(("dp", "fsdp"), None),
            P(("dp", "fsdp")),
            P(("dp", "fsdp"), None),
            P(("dp", "fsdp")),
            P(None, ("dp", "fsdp")),
            P(None, ("dp", "fsdp")),
        ),
        check_vma=False,
    )
```

profile of v0, /device:TPU:0, one launch (start us, length us, event | category | flops | bytes accessed | tf_op | source)
XLA Modules:
  0.0 2344.8 jit_solution(13961418385724998916)
XLA Ops:
  8.1 934.2 %while.46 = (s32[]{:T(128)}, f32[3,768,768]{2,1,0:T(8,128)}, f32[768,768]{1,0:T(8,128)}, f32[3,768,768]{2,1,0:T(8,128)}, f32[768,768]{1,0:T(8,128)}, /*index=5*/...) while((s32[]{:T(128)}, f32[3,768,768]{2,1,0:T(8,128)}, ...), condition=%wide.region_45.46_spmd.clone, body=%wide.region_12.45_spmd.clone.sunk | while | flops 15851543552 | bytes 705414144 | solution.py:477
  14.8 43.9 %all-gather.18 = bf16[32,24,6]{1,2,0:T(8,128)(2,1)S(1)} all-gather(bf16[1,24,6]{1,2,0:T(8,128)(2,1)} %bitcast.575), channel_id=1, replica_groups=mesh['dp'=4,'fsdp'=8] {'dp','fsdp'}, dimensions={0}, use_global_device_ids=true | all-gather | bytes 9504 | tf_op jit(solution)/shard_map/while/body/eval_jaxpr/all_gather | solution.py:312
  136.6 38.4 %all-reduce.23 = (bf16[3072]{0:T(1024)(128)(2,1)S(1)}, bf16[768]{0:T(1024)(128)(2,1)S(1)}) all-reduce(bf16[3072]{0:T(1024)(128)(2,1)S(1)} %dynamic-update-slice.12, bf16[768]{0:T(1024)(128)(2,1)S(1)} %dynamic-update-slice.13), channel_id=1, replica_groups=mesh['dp'=4,'fsdp'=8] {'dp','fsdp'}, use_global_device_ids=true, to_apply=%add.2 | all-reduce | flops 3840 | bytes 15360 | tf_op jit(solution)/shard_map/while
  254.6 60.8 %all-gather.54.cloned.1.call-done = bf16[768,3072]{1,0:T(8,128)(2,1)} async-done(((bf16[24,3072]{1,0:T(8,128)(2,1)}), bf16[768,3072]{1,0:T(8,128)(2,1)}) %all-gather.54.cloned.1.call-update) | async-done | bytes 4718608 | tf_op jit(solution)/shard_map/while/body/eval_jaxpr/all_gather | solution.py:313
  327.6 53.1 %all-gather.56.cloned.1.call-done = bf16[3072,768]{1,0:T(8,128)(2,1)} async-done(((bf16[96,768]{1,0:T(8,128)(2,1)}), bf16[3072,768]{1,0:T(8,128)(2,1)}) %all-gather.56.cloned.1.call-update) | async-done | bytes 4718608 | tf_op jit(solution)/shard_map/while/body/eval_jaxpr/all_gather | solution.py:315
  476.5 39.9 %all-gather.18 = bf16[32,24,6]{1,2,0:T(8,128)(2,1)S(1)} all-gather(bf16[1,24,6]{1,2,0:T(8,128)(2,1)} %bitcast.575), channel_id=1, replica_groups=mesh['dp'=4,'fsdp'=8] {'dp','fsdp'}, dimensions={0}, use_global_device_ids=true | all-gather | bytes 9504 | tf_op jit(solution)/shard_map/while/body/eval_jaxpr/all_gather | solution.py:312
  594.3 38.3 %all-reduce.23 = (bf16[3072]{0:T(1024)(128)(2,1)S(1)}, bf16[768]{0:T(1024)(128)(2,1)S(1)}) all-reduce(bf16[3072]{0:T(1024)(128)(2,1)S(1)} %dynamic-update-slice.12, bf16[768]{0:T(1024)(128)(2,1)S(1)} %dynamic-update-slice.13), channel_id=1, replica_groups=mesh['dp'=4,'fsdp'=8] {'dp','fsdp'}, use_global_device_ids=true, to_apply=%add.2 | all-reduce | flops 3840 | bytes 15360 | tf_op jit(solution)/shard_map/while
  712.2 61.0 %all-gather.54.cloned.1.call-done = bf16[768,3072]{1,0:T(8,128)(2,1)} async-done(((bf16[24,3072]{1,0:T(8,128)(2,1)}), bf16[768,3072]{1,0:T(8,128)(2,1)}) %all-gather.54.cloned.1.call-update) | async-done | bytes 4718608 | tf_op jit(solution)/shard_map/while/body/eval_jaxpr/all_gather | solution.py:313
  796.0 42.5 %all-gather.56.cloned.1.call-done = bf16[3072,768]{1,0:T(8,128)(2,1)} async-done(((bf16[96,768]{1,0:T(8,128)(2,1)}), bf16[3072,768]{1,0:T(8,128)(2,1)}) %all-gather.56.cloned.1.call-update) | async-done | bytes 4718608 | tf_op jit(solution)/shard_map/while/body/eval_jaxpr/all_gather | solution.py:315
  1062.9 59.1 %all-to-all-done = bf16[1,4,8,55296]{3,1,0,2:T(4,128)(2,1)S(1)} async-done(((bf16[1,4,8,55296]{3,1,0,2:T(4,128)(2,1)}), bf16[1,4,8,55296]{3,1,0,2:T(4,128)(2,1)S(1)}, u32[]{:S(2)}, u32[]{:S(2)}) %all-to-all-start) | async-done | bytes 3538976 | tf_op jit(solution)/shard_map/all_to_all | solution.py:332
  1147.5 59.1 %all-to-all-done.2 = bf16[1,4,8,55296]{3,1,0,2:T(4,128)(2,1)} async-done(((bf16[1,4,8,55296]{3,1,0,2:T(4,128)(2,1)}), bf16[1,4,8,55296]{3,1,0,2:T(4,128)(2,1)}, u32[]{:S(2)}, u32[]{:S(2)}) %all-to-all-start.2) | async-done | bytes 3538976 | tf_op jit(solution)/shard_map/all_to_all | solution.py:338
  1231.7 84.8 %all-to-all-done.5 = bf16[1,4,8,73728]{3,1,0,2:T(4,128)(2,1)} async-done(((bf16[1,4,8,73728]{3,1,0,2:T(4,128)(2,1)}), bf16[1,4,8,73728]{3,1,0,2:T(4,128)(2,1)}, u32[]{:S(2)}, u32[]{:S(2)}) %all-to-all-start.5) | async-done | bytes 4718624 | tf_op jit(solution)/shard_map/all_to_all | solution.py:347
  1353.7 72.6 %all-to-all-done.7 = bf16[1,4,8,73728]{3,1,0,2:T(4,128)(2,1)} async-done(((bf16[1,4,8,73728]{3,1,0,2:T(4,128)(2,1)}), bf16[1,4,8,73728]{3,1,0,2:T(4,128)(2,1)}, u32[]{:S(2)}, u32[]{:S(2)}) %all-to-all-start.7) | async-done | bytes 4718624 | tf_op jit(solution)/shard_map/all_to_all | solution.py:353
  1465.2 47.4 %all-reduce.26.cloned.1.call-done = (bf16[3,96,768]{2,0,1:T(4,128)(2,1)}, bf16[3,96,768]{2,0,1:T(4,128)(2,1)}) async-done(((bf16[3,96,768]{2,0,1:T(4,128)(2,1)}, bf16[3,96,768]{2,0,1:T(4,128)(2,1)}), (bf16[3,96,768]{2,0,1:T(4,128)(2,1)}, bf16[3,96,768]{2,0,1:T(4,128)(2,1)})) %all-reduce.26.cloned.1.call-update) | async-done | bytes 884752
  1570.3 766.8 %while.45 = (s32[]{:T(128)}, bf16[2,256,768]{2,1,0:T(8,128)(2,1)}, bf16[2,256,768]{2,1,0:T(8,128)(2,1)S(1)}, bf16[3,24,768]{2,1,0:T(8,128)(2,1)}, bf16[6,24]{1,0...) while((s32[]{:T(128)}, bf16[2,256,768]{2,1,0:T(8,128)(2,1)}, ...), condition=%wide.region_11.12_spmd, body=%wide.region_0.11_spmd.sunk | while | flops 5304690176 | bytes 112198040 | solution.py:465
  1576.8 41.1 %all-gather.15 = bf16[32,24,6]{1,2,0:T(8,128)(2,1)S(1)} all-gather(bf16[1,24,6]{1,2,0:T(8,128)(2,1)} %bitcast.470), channel_id=1, replica_groups=mesh['dp'=4,'fsdp'=8] {'dp','fsdp'}, dimensions={0}, use_global_device_ids=true | all-gather | bytes 9504 | tf_op jit(solution)/shard_map/while/body/eval_jaxpr/all_gather | solution.py:312
  1766.6 42.5 %all-gather.44.cloned.1.call-done = bf16[768,768]{1,0:T(8,128)(2,1)} async-done(((bf16[24,768]{1,0:T(8,128)(2,1)}), bf16[768,768]{1,0:T(8,128)(2,1)}) %all-gather.44.cloned.1.call-update) | async-done | bytes 1179664 | tf_op jit(solution)/shard_map/while/body/eval_jaxpr/all_gather | solution.py:311
  1811.3 63.3 %all-gather.34.cloned.1.call-done = bf16[3072,768]{1,0:T(8,128)(2,1)} async-done(((bf16[96,768]{1,0:T(8,128)(2,1)}), bf16[3072,768]{1,0:T(8,128)(2,1)}) %all-gather.34.cloned.1.call-update) | async-done | bytes 4718608 | tf_op jit(solution)/shard_map/while/body/eval_jaxpr/all_gather | solution.py:315
  1874.6 65.4 %all-gather.36.cloned.1.call-done = bf16[768,3072]{1,0:T(8,128)(2,1)} async-done(((bf16[24,3072]{1,0:T(8,128)(2,1)}), bf16[768,3072]{1,0:T(8,128)(2,1)}) %all-gather.36.cloned.1.call-update) | async-done | bytes 4718608 | tf_op jit(solution)/shard_map/while/body/eval_jaxpr/all_gather | solution.py:313
  1960.9 39.9 %all-gather.15 = bf16[32,24,6]{1,2,0:T(8,128)(2,1)S(1)} all-gather(bf16[1,24,6]{1,2,0:T(8,128)(2,1)} %bitcast.470), channel_id=1, replica_groups=mesh['dp'=4,'fsdp'=8] {'dp','fsdp'}, dimensions={0}, use_global_device_ids=true | all-gather | bytes 9504 | tf_op jit(solution)/shard_map/while/body/eval_jaxpr/all_gather | solution.py:312
  2078.7 38.3 %all-reduce.22 = (bf16[3072]{0:T(1024)(128)(2,1)S(1)}, bf16[768]{0:T(1024)(128)(2,1)S(1)}) all-reduce(bf16[3072]{0:T(1024)(128)(2,1)S(1)} %dynamic-update-slice.10, bf16[768]{0:T(1024)(128)(2,1)S(1)} %dynamic-update-slice.11), channel_id=1, replica_groups=mesh['dp'=4,'fsdp'=8] {'dp','fsdp'}, use_global_device_ids=true, to_apply=%add | all-reduce | flops 3840 | bytes 15360 | tf_op jit(solution)/shard_map/while
  2149.3 42.6 %all-gather.44.cloned.1.call-done = bf16[768,768]{1,0:T(8,128)(2,1)} async-done(((bf16[24,768]{1,0:T(8,128)(2,1)}), bf16[768,768]{1,0:T(8,128)(2,1)}) %all-gather.44.cloned.1.call-update) | async-done | bytes 1179664 | tf_op jit(solution)/shard_map/while/body/eval_jaxpr/all_gather | solution.py:311
  2194.2 63.4 %all-gather.34.cloned.1.call-done = bf16[3072,768]{1,0:T(8,128)(2,1)} async-done(((bf16[96,768]{1,0:T(8,128)(2,1)}), bf16[3072,768]{1,0:T(8,128)(2,1)}) %all-gather.34.cloned.1.call-update) | async-done | bytes 4718608 | tf_op jit(solution)/shard_map/while/body/eval_jaxpr/all_gather | solution.py:315
  2257.6 65.4 %all-gather.36.cloned.1.call-done = bf16[768,3072]{1,0:T(8,128)(2,1)} async-done(((bf16[24,3072]{1,0:T(8,128)(2,1)}), bf16[768,3072]{1,0:T(8,128)(2,1)}) %all-gather.36.cloned.1.call-update) | async-done | bytes 4718608 | tf_op jit(solution)/shard_map/while/body/eval_jaxpr/all_gather | solution.py:313
  (1115 shorter events, 1145.1 us)
Async XLA Ops:
  8.3 174.1 %all-gather.46.cloned.1.call-start = ((), (), s32[]{:S(2)}) async-start(), calls=%async_computation.32 | async-start | bytes 3649536 | tf_op jit(solution)/shard_map/while/body/eval_jaxpr/all_gather | solution.py:308
  9.1 186.1 %all-gather.48.cloned.1.call-start = ((), (), s32[]{:S(2)}) async-start(), calls=%async_computation.33 | async-start | bytes 1216512 | tf_op jit(solution)/shard_map/while/body/eval_jaxpr/all_gather | solution.py:309
  9.8 189.1 %all-gather.50.cloned.1.call-start = ((), (), s32[]{:S(2)}) async-start(), calls=%async_computation.34 | async-start | bytes 3649536 | tf_op jit(solution)/shard_map/while/body/eval_jaxpr/all_gather | solution.py:310
  10.6 239.3 %all-gather.52.cloned.1.call-start = ((), (), s32[]{:S(2)}) async-start(), calls=%async_computation.35 | async-start | bytes 1216512 | tf_op jit(solution)/shard_map/while/body/eval_jaxpr/all_gather | solution.py:311
  11.1 304.2 %all-gather.54.cloned.1.call-start = ((), (), s32[]{:S(2)}) async-start(), calls=%async_computation.36 | async-start | bytes 4866048 | tf_op jit(solution)/shard_map/while/body/eval_jaxpr/all_gather | solution.py:313
  11.7 369.0 %all-gather.56.cloned.1.call-start = ((), (), s32[]{:S(2)}) async-start(), calls=%async_computation.37 | async-start | bytes 4866048 | tf_op jit(solution)/shard_map/while/body/eval_jaxpr/all_gather | solution.py:315
  470.6 182.3 %all-gather.48.cloned.1.call-start = ((), (), s32[]{:S(2)}) async-start(), calls=%async_computation.33 | async-start | bytes 1216512 | tf_op jit(solution)/shard_map/while/body/eval_jaxpr/all_gather | solution.py:309
  471.4 185.2 %all-gather.50.cloned.1.call-start = ((), (), s32[]{:S(2)}) async-start(), calls=%async_computation.34 | async-start | bytes 3649536 | tf_op jit(solution)/shard_map/while/body/eval_jaxpr/all_gather | solution.py:310
  472.1 235.4 %all-gather.52.cloned.1.call-start = ((), (), s32[]{:S(2)}) async-start(), calls=%async_computation.35 | async-start | bytes 1216512 | tf_op jit(solution)/shard_map/while/body/eval_jaxpr/all_gather | solution.py:311
  472.7 300.5 %all-gather.54.cloned.1.call-start = ((), (), s32[]{:S(2)}) async-start(), calls=%async_computation.36 | async-start | bytes 4866048 | tf_op jit(solution)/shard_map/while/body/eval_jaxpr/all_gather | solution.py:313
  473.4 365.1 %all-gather.56.cloned.1.call-start = ((), (), s32[]{:S(2)}) async-start(), calls=%async_computation.37 | async-start | bytes 4866048 | tf_op jit(solution)/shard_map/while/body/eval_jaxpr/all_gather | solution.py:315
  1337.6 175.0 %all-reduce.26.cloned.1.call-start = ((), (), s32[]{:S(2)}) async-start(), calls=%async_computation.25 | async-start | bytes 2359296
  1347.6 192.9 %reduce-scatter.28.cloned.1.call-start = ((), (), s32[]{:S(2)}) async-start(), calls=%async_computation.22 | async-start | bytes 737280
  1353.7 215.0 %reduce-scatter.20.cloned.1.call-start = ((), (), s32[]{:S(2)}) async-start(), calls=%async_computation.18 | async-start | bytes 737280 | tf_op jit(solution)/shard_map/reduce_scatter | solution.py:394
  1571.3 178.3 %all-gather.42.cloned.1.call-start = ((), (), s32[]{:S(2)}) async-start(), calls=%async_computation.30 | async-start | bytes 1216512 | tf_op jit(solution)/shard_map/while/body/eval_jaxpr/all_gather | solution.py:309
  1571.8 181.4 %all-gather.38.cloned.1.call-start = ((), (), s32[]{:S(2)}) async-start(), calls=%async_computation.28 | async-start | bytes 3649536 | tf_op jit(solution)/shard_map/while/body/eval_jaxpr/all_gather | solution.py:310
  1572.4 236.7 %all-gather.44.cloned.1.call-start = ((), (), s32[]{:S(2)}) async-start(), calls=%async_computation.31 | async-start | bytes 1216512 | tf_op jit(solution)/shard_map/while/body/eval_jaxpr/all_gather | solution.py:311
  1573.0 301.6 %all-gather.34.cloned.1.call-start = ((), (), s32[]{:S(2)}) async-start(), calls=%async_computation.26 | async-start | bytes 4866048 | tf_op jit(solution)/shard_map/while/body/eval_jaxpr/all_gather | solution.py:315
  1573.6 366.4 %all-gather.36.cloned.1.call-start = ((), (), s32[]{:S(2)}) async-start(), calls=%async_computation.27 | async-start | bytes 4866048 | tf_op jit(solution)/shard_map/while/body/eval_jaxpr/all_gather | solution.py:313
  1954.9 177.6 %all-gather.42.cloned.1.call-start = ((), (), s32[]{:S(2)}) async-start(), calls=%async_computation.30 | async-start | bytes 1216512 | tf_op jit(solution)/shard_map/while/body/eval_jaxpr/all_gather | solution.py:309
  1955.5 180.4 %all-gather.38.cloned.1.call-start = ((), (), s32[]{:S(2)}) async-start(), calls=%async_computation.28 | async-start | bytes 3649536 | tf_op jit(solution)/shard_map/while/body/eval_jaxpr/all_gather | solution.py:310
  1956.3 235.7 %all-gather.44.cloned.1.call-start = ((), (), s32[]{:S(2)}) async-start(), calls=%async_computation.31 | async-start | bytes 1216512 | tf_op jit(solution)/shard_map/while/body/eval_jaxpr/all_gather | solution.py:311
  1957.0 300.6 %all-gather.34.cloned.1.call-start = ((), (), s32[]{:S(2)}) async-start(), calls=%async_computation.26 | async-start | bytes 4866048 | tf_op jit(solution)/shard_map/while/body/eval_jaxpr/all_gather | solution.py:315
  1957.8 365.2 %all-gather.36.cloned.1.call-start = ((), (), s32[]{:S(2)}) async-start(), calls=%async_computation.27 | async-start | bytes 4866048 | tf_op jit(solution)/shard_map/while/body/eval_jaxpr/all_gather | solution.py:313
  (305 other events, 5534.6 us)
Sparse Core Ops, SparseCore 0:
  12.4 63.1 all-gather.45
  78.5 52.9 all-gather.47
  134.7 59.2 all-gather.49
  196.9 52.9 all-gather.51
  252.7 62.5 all-gather.53
  318.3 62.4 all-gather.55
  473.9 59.2 all-gather.45
  536.2 52.9 all-gather.47
  592.3 59.2 all-gather.49
  654.5 52.9 all-gather.51
  710.5 62.5 all-gather.53
  776.1 62.4 all-gather.55
  1574.5 60.3 all-gather.39
  1637.8 52.9 all-gather.41
  1693.9 59.2 all-gather.37
  1756.1 52.9 all-gather.43
  1812.0 62.5 all-gather.33
  1877.5 62.4 all-gather.35
  1958.2 59.2 all-gather.39
  2020.3 52.9 all-gather.41
  2076.5 59.3 all-gather.37
  2138.9 52.9 all-gather.43
  2195.0 62.5 all-gather.33
  2260.5 62.4 all-gather.35
Sparse Core Ops, SparseCore 1:
  1324.9 23.3 reduce-scatter.29
  1351.6 23.0 reduce-scatter.31
  1377.9 23.0 reduce-scatter.25
  1404.5 23.4 reduce-scatter.21
  1431.5 23.4 reduce-scatter.23
  1458.3 54.2 all-reduce.25
  1515.3 25.1 reduce-scatter.27
  1543.5 25.1 reduce-scatter.19
where the time goes:
time: 2350 us; the launch traced here: 2340 us
  waiting for transfers between devices  1060 us (45%)
  blocking collectives  628 us (27%)
  matrix products  278 us (12%)
  local copies, waits for them, and re-layouts  175 us (7%)
  other arithmetic  119 us (5%)
  starting transfers between devices  44.7 us (2%)
    all_gather x4, waiting for transfers between devices, gather_weights(): lax.all_gather(expand_weight, ('dp', 'fsdp'), axis=0, tiled=True)  253 us
    all_gather x4, waiting for transfers between devices, gather_weights(): lax.all_gather(contract_weight, ('dp', 'fsdp'), axis=0, tiled=True)  222 us
    all_gather x4, blocking collectives, gather_weights(): lax.all_gather(attend_bias, ('dp', 'fsdp'), axis=1, tiled=True)  165 us
    while x4, blocking collectives  153 us
    all_gather x4, blocking collectives, gather_weights(): lax.all_gather(norm_shift, ('dp', 'fsdp'), axis=1, tiled=True)  151 us
    all_gather x4, blocking collectives, gather_weights(): lax.all_gather(norm_gain, ('dp', 'fsdp'), axis=1, tiled=True)  150 us
    all_gather x4, waiting for transfers between devices, gather_weights(): lax.all_gather(cross_output, ('dp', 'fsdp'), axis=0, tiled=True)  150 us
    dot_general x38, matrix products, project(): return jnp.dot(left_side, right_side, preferred_element_type=jnp.float32)  136 us
  transfers between devices with their start and end apart: 43, of which 28 were waited for; matrix products, arithmetic and copies ran while one was open for 15% of the time, Pallas kernels for 0%

commit v1 on v0

v1 whole, which is shorter than its diff:
```python
import functools

import jax
import jax.numpy as jnp
import numpy as np
from jax import lax
from jax.experimental import pallas as pl
from jax.experimental.pallas import tpu as pltpu
from jax.sharding import PartitionSpec as P

D = 768
H = 12
HD = 64
FF = 3072
AXES = ("dp", "fsdp")

EPS = 1e-05
BIG_NEGATIVE = -1000000000.0
HEADS_PER_STEP = 4
BF = jnp.bfloat16
F32 = jnp.float32


class Place:
    def __init__(self):
        self.dp_count = lax.axis_size("dp")
        self.inner = lax.axis_size("fsdp")
        self.chips = self.inner // 2
        self.dp = lax.axis_index("dp")
        inner = lax.axis_index("fsdp")
        self.chip = inner // 2
        self.core = inner % 2
        self.bits = int(np.log2(self.dp_count))

    def bit(self, core, step):
        return 1 << (self.bits - 1 - step if core == 0 else step)

    def mask(self, relative):
        values = [
            sum(self.bit(core, s) for s in range(self.bits) if relative >> s & 1)
            for core in (0, 1)
        ]
        return jnp.where(self.core == 0, values[0], values[1])

    def permute(self, value, target):
        pairs = []
        for dp in range(self.dp_count):
            for chip in range(self.chips):
                for core in range(2):
                    to = target(dp, chip, core)
                    pairs.append(
                        (
                            dp * self.inner + chip * 2 + core,
                            to[0] * self.inner + to[1] * 2 + to[2],
                        )
                    )
        return lax.ppermute(value, AXES, pairs)

    def across_cores(self, value):
        return self.permute(value, lambda d, z, c: (d, z, 1 - c))

    def across_step(self, value, step):
        return self.permute(value, lambda d, z, c: (d ^ self.bit(c, step), z, c))

    def along_chips(self, value, shift):
        return self.permute(value, lambda d, z, c: (d, (z + shift) % self.chips, c))


def owner_blocks(place, gradient):
    rows = gradient.shape[0] // (place.dp_count * place.inner)
    return gradient.reshape(
        place.dp_count, place.chips, 2, rows, gradient.shape[-1]
    )


def reduce_to_owner(place, blocks):
    others = [place.across_cores(b) for b in blocks]

    def chip_sum(where):
        parts = []
        for mine, other in zip(blocks, others):
            shape = (1, place.chips, 1) + mine.shape[3:]
            at = (where, 0, place.core, 0, 0)
            both = lax.dynamic_slice(mine, at, shape).astype(F32) + lax.dynamic_slice(
                other, at, shape
            ).astype(F32)
            parts.append(both.reshape((place.chips,) + mine.shape[3:]))
        return parts[0] if len(parts) == 1 else jnp.concatenate(parts, axis=1)

    arrived = {m: [] for m in range(1 << place.bits)}

    def total(relative):
        value = chip_sum(place.dp ^ place.mask(relative))
        for a in arrived[relative]:
            value = value + a.astype(F32)
        return value

    for step in range(place.bits):
        leaving = [
            m
            for m in range(1 << place.bits)
            if m >> step & 1 and not m & ((1 << step) - 1)
        ]
        sent = jnp.stack([total(m).astype(BF) for m in leaving])
        got = place.across_step(sent, step)
        for i, m in enumerate(leaving):
            arrived[m ^ (1 << step)].append(got[i])
    own = total(0)
    low = own.astype(BF)

    def chip_row(value, shift):
        return lax.dynamic_index_in_dim(
            value, (place.chip + shift) % place.chips, 0, keepdims=False
        )

    result = chip_row(own, 0)
    for shift in range(1, place.chips):
        result = result + place.along_chips(chip_row(low, shift), shift).astype(F32)
    return result


def dot_nt(a, b):
    return lax.dot_general(a, b, (((1,), (1,)), ((), ())), preferred_element_type=F32)


def dot_nn(a, b):
    return jnp.dot(a, b, preferred_element_type=F32)


def dot_tn(a, b):
    return lax.dot_general(a, b, (((0,), (0,)), ((), ())), preferred_element_type=F32)


def attend_kernel(masked, start_ref, length_ref, q_ref, k_ref, v_ref, o_ref, p_ref):
    rows = q_ref.shape[0]
    keys = k_ref.shape[0]
    if masked:
        seq = pl.program_id(0)
        start = start_ref[seq]
        stop = start + length_ref[seq]
        key_at = lax.broadcasted_iota(jnp.int32, (keys, rows), 0)
        row_at = lax.broadcasted_iota(jnp.int32, (keys, rows), 1)
        inside = (key_at >= start) & (key_at < stop) & (row_at >= start) & (row_at < stop)
        allowed = (key_at <= row_at) | inside
    values_t = v_ref[...].T
    pieces = []
    for h in range(HEADS_PER_STEP):
        cols = slice(h * HD, (h + 1) * HD)
        scores = dot_nt(k_ref[:, cols], q_ref[:, cols])
        if masked:
            scores = jnp.where(allowed, scores, BIG_NEGATIVE)
        peak = jnp.max(scores, axis=0, keepdims=True)
        weights = jnp.exp(scores - peak)
        total = jnp.sum(weights, axis=0, keepdims=True)
        low = (weights * (1.0 / total)).astype(BF)
        p_ref[0, h] = low
        pieces.append(dot_nn(values_t[cols], low))
    o_ref[...] = jnp.concatenate(pieces, axis=0).T.astype(BF)


def attend(queries, keys, values, start, length, masked, count):
    rows = queries.shape[0] // count
    key_rows = keys.shape[0] // count
    width = HEADS_PER_STEP * HD
    block = lambda n: pl.BlockSpec((n, width), lambda s, g, *_: (s, g))
    return pl.pallas_call(
        functools.partial(attend_kernel, masked),
        grid_spec=pltpu.PrefetchScalarGridSpec(
            num_scalar_prefetch=2,
            grid=(count, H // HEADS_PER_STEP),
            in_specs=[block(rows), block(key_rows), block(key_rows)],
            out_specs=[
                block(rows),
                pl.BlockSpec(
                    (1, HEADS_PER_STEP, key_rows, rows), lambda s, g, *_: (s, g, 0, 0)
                ),
            ],
        ),
        out_shape=[
            jax.ShapeDtypeStruct(queries.shape, BF),
            jax.ShapeDtypeStruct((count, H, key_rows, rows), BF),
        ],
        compiler_params=pltpu.CompilerParams(vmem_limit_bytes=24 << 20),
        name="attend",
    )(start, length, queries, keys, values)


def attend_back_kernel(q_ref, k_ref, v_ref, p_ref, g_ref, dq_ref, dk_ref, dv_ref):
    keys_t = k_ref[...].T
    dq, dk, dv = [], [], []
    for h in range(HEADS_PER_STEP):
        cols = slice(h * HD, (h + 1) * HD)
        grads = g_ref[:, cols]
        low = p_ref[0, h]
        weights = low.astype(F32)
        moved = dot_nt(v_ref[:, cols], grads)
        centre = jnp.sum(weights * moved, axis=0, keepdims=True)
        ds = (weights * (moved - centre)).astype(BF)
        dk.append(dot_nn(ds, q_ref[:, cols]))
        dv.append(dot_nn(low, grads))
        dq.append(dot_nn(keys_t[cols], ds))
    dq_ref[...] = jnp.concatenate(dq, axis=0).T.astype(BF)
    dk_ref[...] = jnp.concatenate(dk, axis=1).astype(BF)
    dv_ref[...] = jnp.concatenate(dv, axis=1).astype(BF)


def attend_back(queries, keys, values, weights, grads, count):
    rows = queries.shape[0] // count
    key_rows = keys.shape[0] // count
    width = HEADS_PER_STEP * HD
    block = lambda n: pl.BlockSpec((n, width), lambda s, g: (s, g))
    return pl.pallas_call(
        attend_back_kernel,
        grid=(count, H // HEADS_PER_STEP),
        in_specs=[
            block(rows),
            block(key_rows),
            block(key_rows),
            pl.BlockSpec((1, HEADS_PER_STEP, key_rows, rows), lambda s, g: (s, g, 0, 0)),
            block(rows),
        ],
        out_specs=[block(rows), block(key_rows), block(key_rows)],
        out_shape=[
            jax.ShapeDtypeStruct(queries.shape, BF),
            jax.ShapeDtypeStruct(keys.shape, BF),
            jax.ShapeDtypeStruct(keys.shape, BF),
        ],
        compiler_params=pltpu.CompilerParams(vmem_limit_bytes=24 << 20),
        name="attend_back",
    )(queries, keys, values, weights, grads)


def norm(summed):
    centre = summed - jnp.mean(summed, axis=-1, keepdims=True)
    scale = lax.rsqrt(jnp.mean(centre * centre, axis=-1, keepdims=True) + EPS)
    return centre * scale, scale


def norm_back(normal, scale, gain, grad):
    inner = grad * gain
    back = scale * (
        inner
        - jnp.mean(inner, axis=-1, keepdims=True)
        - normal * jnp.mean(inner * normal, axis=-1, keepdims=True)
    )
    return back, jnp.sum(grad * normal, axis=0), jnp.sum(grad, axis=0)


def gelu_and_slope(value):
    spread = 0.5 * (1.0 + lax.erf(value * np.float32(np.sqrt(0.5))))
    density = jnp.exp(-0.5 * value * value) * np.float32(1.0 / np.sqrt(2.0 * np.pi))
    return value * spread, spread + value * density


def gather_weights(shards):
    (sp, so, cp, co, ab, ew, eb, cw, cb, ng, ns) = shards
    rows = so.shape[0]
    small = jnp.concatenate([a.reshape(-1) for a in (ab, eb, cb, ng, ns)])
    used = small.shape[0]
    small = jnp.pad(small, (0, 8 * D - used)).reshape(8, D)
    packed = jnp.concatenate(
        [
            sp.reshape(-1, D),
            so,
            cp.reshape(-1, D),
            co,
            ew.reshape(rows, FF // D, D).swapaxes(0, 1).reshape(-1, D),
            cw,
            small,
        ]
    )
    whole = lax.all_gather(packed, AXES, axis=0, tiled=False)
    count = whole.shape[0]

    def square(i):
        return whole[:, i * rows : (i + 1) * rows].reshape(D, D)

    squares = [square(i) for i in range(12)]
    contract = whole[:, 12 * rows : 12 * rows + cw.shape[0]].reshape(FF, D)
    tail = whole[:, 12 * rows + cw.shape[0]].astype(F32)
    at = 0
    smalls = []
    for a in (ab, eb, cb, ng, ns):
        piece = tail[:, at : at + a.size].reshape((count,) + a.shape)
        at += a.size
        smalls.append(
            piece.reshape(-1) if a.ndim == 1 else piece.swapaxes(0, 1).reshape(a.shape[0], -1)
        )
    return squares, contract, smalls


def body(
    layer_input,
    encoder_states,
    output_grad,
    span_start,
    span_length,
    self_project,
    self_output,
    cross_project,
    cross_output,
    attend_bias,
    expand_weight,
    expand_bias,
    contract_weight,
    contract_bias,
    norm_gain,
    norm_shift,
):
    place = Place()
    count, length = layer_input.shape[:2]
    shape = layer_input.shape
    x = layer_input.reshape(-1, D)
    memory = encoder_states.reshape(-1, D)
    grad_out = output_grad.reshape(-1, D).astype(F32)
    squares, contract, smalls = gather_weights(
        (
            self_project,
            self_output,
            cross_project,
            cross_output,
            attend_bias,
            expand_weight,
            expand_bias,
            contract_weight,
            contract_bias,
            norm_gain,
            norm_shift,
        )
    )
    wq, wk, wv, wo, cq, ck, cv, co = squares[:8]
    expand = jnp.concatenate(squares[8:], axis=1)
    biases, expand_b, contract_b, gains, shifts = smalls

    q = ((dot_nn(x, wq) + biases[0]) * 0.125).astype(BF)
    k = dot_nn(x, wk).astype(BF)
    v = (dot_nn(x, wv) + biases[1]).astype(BF)
    o, p = attend(q, k, v, span_start, span_length, True, count)
    n1, s1 = norm(x.astype(F32) + (dot_nn(o, wo) + biases[2]))
    x1 = n1 * gains[0] + shifts[0]
    x1b = x1.astype(BF)
    q2 = ((dot_nn(x1b, cq) + biases[3]) * 0.125).astype(BF)
    k2 = dot_nn(memory, ck).astype(BF)
    v2 = (dot_nn(memory, cv) + biases[4]).astype(BF)
    o2, p2 = attend(q2, k2, v2, span_start, span_length, False, count)
    n2, s2 = norm(x1 + (dot_nn(o2, co) + biases[5]))
    x2 = n2 * gains[1] + shifts[1]
    x2b = x2.astype(BF)
    act, slope = gelu_and_slope(dot_nn(x2b, expand) + expand_b)
    act = act.astype(BF)
    slope = slope.astype(BF)
    n3, s3 = norm(x2 + (dot_nn(act, contract) + contract_b))
    output = (n3 * gains[2] + shifts[2]).astype(BF)

    dr3, gain3, shift3 = norm_back(n3, s3, gains[2], grad_out)
    df = dr3.astype(BF)
    d_contract = dot_tn(act, df).astype(BF)
    d_contract_b = jnp.sum(df.astype(F32), axis=0)
    du = (dot_nt(df, contract) * slope.astype(F32)).astype(BF)
    d_expand = dot_tn(x2b, du).astype(BF)
    d_expand_b = jnp.sum(du.astype(F32), axis=0)
    own_contract = reduce_to_owner(place, [owner_blocks(place, d_contract)])
    own_expand = reduce_to_owner(place, [owner_blocks(place, d_expand)])

    dr2, gain2, shift2 = norm_back(n2, s2, gains[1], dr3 + dot_nt(du, expand))
    dc = dr2.astype(BF)
    d_co = dot_tn(o2, dc).astype(BF)
    do2 = dot_nt(dc, co).astype(BF)
    dq2, dk2, dv2 = attend_back(q2, k2, v2, p2, do2, count)
    dq2 = dq2 * BF(0.125)
    d_cross = [dot_tn(x1b, dq2), dot_tn(memory, dk2), dot_tn(memory, dv2)]
    own_cross = reduce_to_owner(
        place, [owner_blocks(place, d.astype(BF)) for d in d_cross + [d_co]]
    )
    encoder_grad = dot_nt(dk2, ck) + dot_nt(dv2, cv)

    dr1, gain1, shift1 = norm_back(n1, s1, gains[0], dr2 + dot_nt(dq2, cq))
    da = dr1.astype(BF)
    d_so = dot_tn(o, da).astype(BF)
    do = dot_nt(da, wo).astype(BF)
    dq, dk, dv = attend_back(q, k, v, p, do, count)
    dq = dq * BF(0.125)
    d_self = [dot_tn(x, dq), dot_tn(x, dk), dot_tn(x, dv)]
    input_grad = dr1 + dot_nt(dq, wq) + dot_nt(dk, wk) + dot_nt(dv, wv)

    def column_sum(value):
        return jnp.sum(value.astype(F32), axis=0)

    d_bias = jnp.stack(
        [column_sum(t) for t in (dq, dv, da, dq2, dv2, dc)]
    )
    smalls_out = [
        d_bias,
        d_expand_b,
        d_contract_b,
        jnp.stack([gain1, gain2, gain3]),
        jnp.stack([shift1, shift2, shift3]),
    ]
    devices = place.dp_count * place.inner
    flat = []
    for s in smalls_out:
        by_owner = s.reshape(s.shape[:-1] + (devices, -1))
        flat.append(jnp.moveaxis(by_owner, -2, 0).reshape(devices, -1))
    flat = jnp.concatenate(flat, axis=1)
    flat = jnp.pad(flat, ((0, 0), (0, 8 * D - flat.shape[1]))).astype(BF)
    small_blocks = flat.reshape(place.dp_count, place.chips, 2, 8, D)
    own_self = reduce_to_owner(
        place,
        [owner_blocks(place, d.astype(BF)) for d in d_self + [d_so]] + [small_blocks],
    )
    rows = self_output.shape[0]
    tail = own_self[4 * rows]
    at = 0
    own_small = []
    for a in (attend_bias, expand_bias, contract_bias, norm_gain, norm_shift):
        own_small.append(tail[at : at + a.size].reshape(a.shape))
        at += a.size
    return (
        output.reshape(shape),
        input_grad.reshape(shape),
        encoder_grad.reshape(encoder_states.shape),
        own_self[: 3 * rows].reshape(3, rows, D),
        own_self[3 * rows : 4 * rows],
        own_cross[: 3 * rows].reshape(3, rows, D),
        own_cross[3 * rows :],
        own_small[0],
        own_expand,
        own_small[1],
        own_contract,
        own_small[2],
        own_small[3],
        own_small[4],
    )


def solution(mesh):
    rows = P(AXES)
    return jax.shard_map(
        body,
        mesh=mesh,
        in_specs=(
            P(AXES, None, None),
            P(AXES, None, None),
            P(AXES, None, None),
            P(AXES),
            P(AXES),
            P(None, AXES, None),
            P(AXES, None),
            P(None, AXES, None),
            P(AXES, None),
            P(None, AXES),
            P(AXES, None),
            P(AXES),
            P(AXES, None),
            P(AXES),
            P(None, AXES),
            P(None, AXES),
        ),
        out_specs=(
            P(AXES, None, None),
            P(AXES, None, None),
            P(AXES, None, None),
            P(None, AXES, None),
            P(AXES, None),
            P(None, AXES, None),
            P(AXES, None),
            P(None, AXES),
            P(AXES, None),
            P(AXES),
            P(AXES, None),
            P(AXES),
            P(None, AXES),
            P(None, AXES),
        ),
        check_vma=False,
    )
```

time: 2350 us -> 482 us (0.21)
  waiting for transfers between devices: 1060 us -> 193 us
  blocking collectives: 628 us -> 0 us
  matrix products: 278 us -> 63.7 us
  local copies, waits for them, and re-layouts: 175 us -> 91.4 us
  other arithmetic: 119 us -> 36.1 us
  Pallas kernels: 0 us -> 39.5 us
    all_gather x24 -> x1, waiting for transfers between devices: 627 us -> 128 us  [gather_weights(): whole = lax.all_gather(packed, AXES, axis=0, tiled=False)]
    all_gather x12 -> x0, blocking collectives: 466 us -> none  [the longest x4 165 us: gather_weights(): lax.all_gather(attend_bias, ('dp', 'fsdp'), axis=1, tiled=True)]
    all_to_all x11 -> x0, waiting for transfers between devices: 322 us -> none  [the longest x1 84.8 us: reduce_grads(): lax.all_to_all(packed[5].astype(jnp.bfloat16), 'fsdp', split_axis=2, conc...]
    dot_general x106 -> x30, matrix products: 267 us -> 63.7 us  [the longest x10 24.2 us: dot_nt(): lax.dot_general(a, b, (((1,), (1,)), ((), ())), preferred_element_type=F32)]
    while x4 -> x0, blocking collectives: 153 us -> none
    convert_element_type x90 -> x0, local copies, waits for them, and re-layouts: 117 us -> none  [the longest x3 20.8 us: reduce_grads(): packed[2].astype(jnp.bfloat16)]
    unnamed x15 -> x1, waiting for transfers between devices: 72.1 us -> 0.02 us
    ppermute x0 -> x31, waiting for transfers between devices: none -> 64.1 us  [permute(): return lax.ppermute(value, AXES, pairs)]
  transfers between devices with their start and end apart: 43 -> 32, of which waited for: 28 -> 10; matrix products, arithmetic and copies ran while one was open for 15% -> 9% of each run, Pallas kernels for 0% -> 0%
where the time goes in v1:
time: 482 us; the launch traced here: 473 us
  waiting for transfers between devices  193 us (40%)
  local copies, waits for them, and re-layouts  91.4 us (19%)
  matrix products  63.7 us (13%)
  Pallas kernels  39.5 us (8%)
  other arithmetic  36.1 us (7%)
  starting transfers between devices  34.1 us (7%)
  between operations  15.6 us (3%)
    all_gather x1, waiting for transfers between devices, gather_weights(): whole = lax.all_gather(packed, AXES, axis=0, tiled=False)  128 us
    ppermute x31, waiting for transfers between devices, permute(): return lax.ppermute(value, AXES, pairs)  64.1 us
    ppermute x31, starting transfers between devices, permute(): return lax.ppermute(value, AXES, pairs)  34.1 us
    dot_general x10, matrix products, dot_nt(): lax.dot_general(a, b, (((1,), (1,)), ((), ())), preferred_element_type=F32)  24.2 us
    dot_general x10, matrix products, dot_tn(): lax.dot_general(a, b, (((0,), (0,)), ((), ())), preferred_element_type=F32)  23.3 us
    unnamed x188, local copies, waits for them, and re-layouts  21.5 us
    pallas_call x2, Pallas kernels, attend(): pl.pallas_call(functools.partial(attend_kernel, masked), grid_spec=pltpu....  20.7 us
    pallas_call x2, Pallas kernels, attend_back(): pl.pallas_call(attend_back_kernel, grid=(count, H // HEADS_PER_STEP), in_...  18.8 us
  transfers between devices with their start and end apart: 32, of which 10 were waited for; matrix products, arithmetic and copies ran while one was open for 9% of the time, Pallas kernels for 0%

profile of v1, /device:TPU:0, one launch (start us, length us, event | category | flops | bytes accessed | tf_op | source)
XLA Modules:
  0.0 472.9 jit_solution(17599491909595135544)
XLA Ops:
  18.2 128.4 %all-gather.3.cloned.1.call-done = bf16[12544,768]{1,0:T(8,128)(2,1)} async-done(((bf16[392,768]{1,0:T(8,128)(2,1)}), bf16[12544,768]{1,0:T(8,128)(2,1)}) %all-gather.3.cloned.1.call-update) | async-done | bytes 19267600 | tf_op jit(solution)/shard_map/all_gather | solution.py:272
  147.9 4.8 %slice.251 = bf16[32,96,768]{2,1,0:T(8,128)(2,1)} slice(bf16[32,392,768]{2,1,0:T(8,128)(2,1)} %bitcast.375), slice={[0:32], [288:384], [0:768]} | slice | bytes 9437184 | tf_op jit(solution)/shard_map/slice | solution.py:279
  152.7 10.1 %fusion.100 = (bf16[32,24,768]{2,1,0:T(8,128)(2,1)}, bf16[32,24,768]{2,1,0:T(8,128)(2,1)}, bf16[32,24,768]{2,1,0:T(8,128)(2,1)}, bf16[32,24,768]{2,1,0:T(8,128)(...) fusion(bf16[32,392,768]{2,1,0:T(8,128)(2,1)} %bitcast.376), kind=kLoop, calls=%fused_computation.261 | loop fusion | bytes 28311552 | tf_op jit(solution)/shard_map/slice | solution.py:276
  176.4 10.3 %attend.2 = (bf16[512,768]{1,0:T(8,128)(2,1)S(1)}, bf16[2,12,256,256]{3,2,1,0:T(8,128)(2,1)S(1)}) custom-call(s32[2]{0:T(128)S(1)} %copy-done.13, s32[2]{0:T(128)S(1)} %copy-done.14, bf16[512,768]{1,0:T(8,128)(2,1)S(1)} %fusion.14.q_ref, bf16[512,768]{1,0:T(8,128)(2,1)S(1)} %fusion.17.k_ref, bf16[512,768]{1,0:T(8,128)(2,1)S(1)} %fusion.15.v_ref), custom_call_target="tpu_custom_call" | custom-call | tf_op jit(solution)/shard_map/attend/pallas_call | solution.py:166
  193.9 10.4 %attend.3 = (bf16[512,768]{1,0:T(8,128)(2,1)S(1)}, bf16[2,12,256,256]{3,2,1,0:T(8,128)(2,1)S(1)}) custom-call(s32[2]{0:T(128)S(1)} %copy-done.13, s32[2]{0:T(128)S(1)} %copy-done.14, bf16[512,768]{1,0:T(8,128)(2,1)S(1)} %multiply_convert_fusion.2.q_ref, bf16[512,768]{1,0:T(8,128)(2,1)S(1)} %fusion.18.k_ref, bf16[512,768]{1,0:T(8,128)(2,1)S(1)} %fusion.16.v_ref), custom_call_target="tpu_custom_call" | custom-call | tf_op jit(solution)/shard_map/attend/pallas_call | solution.py:166
  207.2 5.5 %multiply_convert_fusion.1 = (bf16[512,3072]{1,0:T(8,128)(2,1)S(1)}, f32[512,3072]{1,0:T(8,128)}) fusion(f32[3072]{0:T(1024)S(1)} %copy-done.68, bf16[768,768]{1,0:T(8,128)(2,1)S(1)} %bitcast.435, bf16[768,768]{1,0:T(8,128)(2,1)S(1)} %bitcast.437, bf16[768,768]{1,0:T(8,128)(2,1)S(1)} %bitcast.439, bf16[768,768]{1,0:T(8,128)(2,1)S(1)} %bitcast.441, ...), kind=kOutput, calls=%fused_computation.7 | convolution fusion | flops 2446196736 | bytes 15751168 | tf_op jit(solution)/shard_map/dot_general | solution.py:127
  212.7 2.7 fusion.107
  219.1 4.3 convolution_convert_fusion
  223.4 7.2 %fusion.108 = (bf16[3072]{0:T(1024)(128)(2,1)}, bf16[512,3072]{1,0:T(8,128)(2,1)S(1)}) fusion(f32[512,3072]{1,0:T(8,128)} %get-tuple-element.133, f32[3072]{0:T(1024)S(1)} %copy-done.68, bf16[3072,768]{1,0:T(8,128)(2,1)S(1)} %bitcast.400, f32[512,768]{1,0:T(8,128)S(1)} %get-tuple-element.55), kind=kOutput, calls=%fused_computation.269 | convolution fusion | flops 2438329344 | bytes 15747072 | tf_op jit(solution)/shard_map/dot_general | solution.py:123
  230.6 3.6 multiply_reduce_fusion
  234.2 4.9 %convolution_convert_fusion.1 = bf16[768,3072]{1,0:T(8,128)(2,1)} fusion(bf16[512,3072]{1,0:T(8,128)(2,1)S(1)} %get-tuple-element.139, f32[512,768]{1,0:T(8,128)S(1)} %get-tuple-element.131, f32[768]{0:T(1024)S(1)} %copy-done.72, f32[768]{0:T(1024)S(1)} %mul.206, f32[512]{0:T(512)S(1)} %add_rsqrt_fusion.1, f32[512]{0:T(512)S(1)} %broadcast_multiply_fusion.6), kind=kOutput, calls=%fused_computation.10 | convolution fusion | flops 2420244480 | bytes 9447424 | tf_op jit(solution)/shard_map/dot_general | solution.py:131
  240.7 9.5 %attend_back.2 = (bf16[512,768]{1,0:T(8,128)(2,1)S(1)}, bf16[512,768]{1,0:T(8,128)(2,1)S(1)}, bf16[512,768]{1,0:T(8,128)(2,1)S(1)}) custom-call(bf16[512,768]{1,0:T(8,128)(2,1)S(1)} %multiply_convert_fusion.2.q_ref, bf16[512,768]{1,0:T(8,128)(2,1)S(1)} %fusion.18.k_ref, bf16[512,768]{1,0:T(8,128)(2,1)S(1)} %fusion.16.v_ref, ...), custom_call_target="tpu_custom_call" | custom-call | tf_op jit(solution)/shard_map/attend_back/pallas_call | solution.py:212
  268.7 9.2 %attend_back.3 = (bf16[512,768]{1,0:T(8,128)(2,1)S(1)}, bf16[512,768]{1,0:T(8,128)(2,1)S(1)}, bf16[512,768]{1,0:T(8,128)(2,1)S(1)}) custom-call(bf16[512,768]{1,0:T(8,128)(2,1)S(1)} %copy-done.4, bf16[512,768]{1,0:T(8,128)(2,1)S(1)} %fusion.17.k_ref, bf16[512,768]{1,0:T(8,128)(2,1)S(1)} %fusion.15.v_ref, bf16[2,12,256,256]{3,2,1,0:T(8,128)(2,1)S(1)} %copy-done.2, ...), custom_call_target="tpu_custom_call" | custom-call | tf_op jit(solution)/shard_map/attend_back/pallas_call | solution.py:212
  332.3 3.3 copy.304
  353.5 10.6 %collective-permute-done.14 = bf16[2,4,96,768]{3,2,1,0:T(8,128)(2,1)S(1)} collective-permute-done((bf16[2,4,96,768]{3,2,1,0:T(8,128)(2,1)S(1)}, bf16[2,4,96,768]{3,2,1,0:T(8,128)(2,1)S(1)}, u32[]{:S(2)}, u32[]{:S(2)}) %collective-permute-start.14) | collective-permute-done | bytes 1179680 | tf_op jit(solution)/shard_map/ppermute | solution.py:57
  365.7 18.4 %collective-permute-done.5 = bf16[2,4,104,768]{3,2,1,0:T(8,128)(2,1)S(1)} collective-permute-done((bf16[2,4,104,768]{3,2,1,0:T(8,128)(2,1)S(1)}, bf16[2,4,104,768]{3,2,1,0:T(8,128)(2,1)S(1)}, u32[]{:S(2)}, u32[]{:S(2)}) %collective-permute-start.5) | collective-permute-done | bytes 1277984 | tf_op jit(solution)/shard_map/ppermute | solution.py:57
  386.2 3.9 collective-permute-start.18
  390.1 4.6 collective-permute-done.6
  403.3 2.9 collective-permute-start.9
  411.6 4.7 collective-permute-done.8
  423.4 8.9 %collective-permute-done.20 = bf16[2,4,24,3072]{3,2,1,0:T(8,128)(2,1)S(1)} collective-permute-done((bf16[2,4,24,3072]{3,2,1,0:T(8,128)(2,1)}, bf16[2,4,24,3072]{3,2,1,0:T(8,128)(2,1)S(1)}, u32[]{:S(2)}, u32[]{:S(2)}) %collective-permute-start.20) | collective-permute-done | bytes 1179680 | tf_op jit(solution)/shard_map/ppermute | solution.py:57
  445.4 2.8 collective-permute-start.22
  451.2 9.3 %collective-permute-done.29 = bf16[96,768]{1,0:T(8,128)(2,1)S(1)} collective-permute-done((bf16[96,768]{1,0:T(8,128)(2,1)S(1)}, bf16[96,768]{1,0:T(8,128)(2,1)S(1)}, u32[]{:S(2)}, u32[]{:S(2)}) %collective-permute-start.29) | collective-permute-done | bytes 147488 | tf_op jit(solution)/shard_map/ppermute | solution.py:57
  461.4 3.7 collective-permute-done.23
  (424 shorter events, 173.3 us)
Async XLA Ops:
  7.2 139.4 %all-gather.3.cloned.1.call-start = ((), (), s32[]{:S(2)}) async-start(), calls=%async_computation | async-start | bytes 19869696 | tf_op jit(solution)/shard_map/all_gather | solution.py:272
  320.7 18.8 %collective-permute-start.12 = (bf16[4,4,2,24,768]{4,3,1,2,0:T(8,128)(2,1)}, bf16[4,4,2,24,768]{4,3,1,2,0:T(8,128)(2,1)}, u32[]{:S(2)}, u32[]{:S(2)}) collective-permute-start(bf16[4,4,2,24,768]{4,3,1,2,0:T(8,128)(2,1)} %copy.288), channel_id=1, source_target_pairs={{0,1},{1,0},{2,3},{3,2},{4,5},{5,4},{6,7},{7,6},{8,9},{9,8},{10,11... | collective-permute-start | bytes 3538952 | tf_op jit(solution)/shard_map/ppermute | solution.py:57
  321.0 20.1 %collective-permute-start.11 = (bf16[4,4,2,24,768]{4,3,1,2,0:T(8,128)(2,1)}, bf16[4,4,2,24,768]{4,3,1,2,0:T(8,128)(2,1)}, u32[]{:S(2)}, u32[]{:S(2)}) collective-permute-start(bf16[4,4,2,24,768]{4,3,1,2,0:T(8,128)(2,1)} %copy.286), channel_id=1, source_target_pairs={{0,1},{1,0},{2,3},{3,2},{4,5},{5,4},{6,7},{7,6},{8,9},{9,8},{10,11... | collective-permute-start | bytes 3538952 | tf_op jit(solution)/shard_map/ppermute | solution.py:57
  321.2 24.5 %collective-permute-start.13 = (bf16[4,4,2,24,768]{4,3,1,2,0:T(8,128)(2,1)}, bf16[4,4,2,24,768]{4,3,1,2,0:T(8,128)(2,1)}, u32[]{:S(2)}, u32[]{:S(2)}) collective-permute-start(bf16[4,4,2,24,768]{4,3,1,2,0:T(8,128)(2,1)} %copy.290), channel_id=1, source_target_pairs={{0,1},{1,0},{2,3},{3,2},{4,5},{5,4},{6,7},{7,6},{8,9},{9,8},{10,11... | collective-permute-start | bytes 3538952 | tf_op jit(solution)/shard_map/ppermute | solution.py:57
  321.5 21.3 %collective-permute-start.10 = (bf16[4,4,2,24,768]{4,3,1,2,0:T(8,128)(2,1)}, bf16[4,4,2,24,768]{4,3,1,2,0:T(8,128)(2,1)}, u32[]{:S(2)}, u32[]{:S(2)}) collective-permute-start(bf16[4,4,2,24,768]{4,3,1,2,0:T(8,128)(2,1)} %copy.284), channel_id=1, source_target_pairs={{0,1},{1,0},{2,3},{3,2},{4,5},{5,4},{6,7},{7,6},{8,9},{9,8},{10,11... | collective-permute-start | bytes 3538952 | tf_op jit(solution)/shard_map/ppermute | solution.py:57
  321.7 22.6 %collective-permute-start = (bf16[4,4,2,24,768]{4,3,1,2,0:T(8,128)(2,1)}, bf16[4,4,2,24,768]{4,3,1,2,0:T(8,128)(2,1)}, u32[]{:S(2)}, u32[]{:S(2)}) collective-permute-start(bf16[4,4,2,24,768]{4,3,1,2,0:T(8,128)(2,1)} %copy.258), channel_id=1, source_target_pairs={{0,1},{1,0},{2,3},{3,2},{4,5},{5,4},{6,7},{7,6},{8,9},{9,8},{10,11... | collective-permute-start | bytes 3538952 | tf_op jit(solution)/shard_map/ppermute | solution.py:57
  345.7 50.7 %collective-permute-start.25 = (bf16[4,4,2,96,768]{4,3,1,2,0:T(8,128)(2,1)S(1)}, bf16[4,4,2,96,768]{4,3,1,2,0:T(8,128)(2,1)S(1)}, u32[]{:S(2)}, u32[]{:S(2)}) collective-permute-start(bf16[4,4,2,96,768]{4,3,1,2,0:T(8,128)(2,1)S(1)} %copy.309), channel_id=1, source_target_pairs={{0,1},{1,0},{2,3},{3,2},{4,5},{5,4},{6,7},{7,6},{8,9},{9,8},{10,11... | collective-permute-start | bytes 14155784 | tf_op jit(solution)/shard_map/ppermute | solution.py:57
  347.3 51.6 %collective-permute-start.19 = (bf16[4,4,2,24,3072]{4,3,1,2,0:T(8,128)(2,1)S(1)}, bf16[4,4,2,24,3072]{4,3,1,2,0:T(8,128)(2,1)S(1)}, u32[]{:S(2)}, u32[]{:S(2)}) collective-permute-start(bf16[4,4,2,24,3072]{4,3,1,2,0:T(8,128)(2,1)S(1)} %copy.304), channel_id=1, source_target_pairs={{0,1},{1,0},{2,3},{3,2},{4,5},{5,4},{6,7},{7,6},{8,9},{9,8},{10,11... | collective-permute-start | bytes 14155784 | tf_op jit(solution)/shard_map/ppermute | solution.py:57
  347.8 16.3 %collective-permute-start.14 = (bf16[2,4,96,768]{3,2,1,0:T(8,128)(2,1)S(1)}, bf16[2,4,96,768]{3,2,1,0:T(8,128)(2,1)S(1)}, u32[]{:S(2)}, u32[]{:S(2)}) collective-permute-start(bf16[2,4,96,768]{3,2,1,0:T(8,128)(2,1)S(1)} %maximum_maximum_fusion), channel_id=1, source_target_pairs={{0,16},{1,9},{2,18},{3,11},{4,20},{5,13},{6,22},{7,15},{8,24},{9,1... | collective-permute-start | bytes 3538952 | tf_op jit(solution)/shard_map/ppermute | solution.py:57
  349.7 34.4 %collective-permute-start.5 = (bf16[2,4,104,768]{3,2,1,0:T(8,128)(2,1)S(1)}, bf16[2,4,104,768]{3,2,1,0:T(8,128)(2,1)S(1)}, u32[]{:S(2)}, u32[]{:S(2)}) collective-permute-start(bf16[2,4,104,768]{3,2,1,0:T(8,128)(2,1)S(1)} %pad_maximum_fusion.1), channel_id=1, source_target_pairs={{0,16},{1,9},{2,18},{3,11},{4,20},{5,13},{6,22},{7,15},{8,24},{9,1... | collective-permute-start | bytes 3833864 | tf_op jit(solution)/shard_map/ppermute | solution.py:57
  364.2 21.6 %collective-permute-start.15 = (bf16[1,4,96,768]{3,2,1,0:T(8,128)(2,1)S(1)}, bf16[1,4,96,768]{3,2,1,0:T(8,128)(2,1)S(1)}, u32[]{:S(2)}, u32[]{:S(2)}) collective-permute-start(bf16[1,4,96,768]{3,2,1,0:T(8,128)(2,1)S(1)} %fusion.20), channel_id=1, source_target_pairs={{0,8},{1,17},{2,10},{3,19},{4,12},{5,21},{6,14},{7,23},{8,0},{9,25... | collective-permute-start | bytes 1769480 | tf_op jit(solution)/shard_map/ppermute | solution.py:57
  386.1 17.3 %collective-permute-start.16 = (bf16[96,768]{1,0:T(8,128)(2,1)S(1)}, bf16[96,768]{1,0:T(8,128)(2,1)S(1)}, u32[]{:S(2)}, u32[]{:S(2)}) collective-permute-start(bf16[96,768]{1,0:T(8,128)(2,1)S(1)} %get-tuple-element.111), channel_id=1, source_target_pairs={{0,2},{1,3},{2,4},{3,5},{4,6},{5,7},{6,0},{7,1},{8,10},{9,11},{10,... | collective-permute-start | bytes 442376 | tf_op jit(solution)/shard_map/ppermute | solution.py:57
  386.2 20.0 %collective-permute-start.18 = (bf16[96,768]{1,0:T(8,128)(2,1)S(1)}, bf16[96,768]{1,0:T(8,128)(2,1)S(1)}, u32[]{:S(2)}, u32[]{:S(2)}) collective-permute-start(bf16[96,768]{1,0:T(8,128)(2,1)S(1)} %get-tuple-element.112), channel_id=1, source_target_pairs={{0,6},{1,7},{2,0},{3,1},{4,2},{5,3},{6,4},{7,5},{8,14},{9,15},{10,... | collective-permute-start | bytes 442376 | tf_op jit(solution)/shard_map/ppermute | solution.py:57
  394.7 13.6 %collective-permute-start.17 = (bf16[96,768]{1,0:T(8,128)(2,1)S(1)}, bf16[96,768]{1,0:T(8,128)(2,1)S(1)}, u32[]{:S(2)}, u32[]{:S(2)}) collective-permute-start(bf16[96,768]{1,0:T(8,128)(2,1)S(1)} %get-tuple-element.113), channel_id=1, source_target_pairs={{0,4},{1,5},{2,6},{3,7},{4,0},{5,1},{6,2},{7,3},{8,12},{9,13},{10,... | collective-permute-start | bytes 442376 | tf_op jit(solution)/shard_map/ppermute | solution.py:57
  396.5 15.2 %collective-permute-start.7 = (bf16[104,768]{1,0:T(8,128)(2,1)S(1)}, bf16[104,768]{1,0:T(8,128)(2,1)S(1)}, u32[]{:S(2)}, u32[]{:S(2)}) collective-permute-start(bf16[104,768]{1,0:T(8,128)(2,1)S(1)} %get-tuple-element.102), channel_id=1, source_target_pairs={{0,2},{1,3},{2,4},{3,5},{4,6},{5,7},{6,0},{7,1},{8,10},{9,11},{10,... | collective-permute-start | bytes 479240 | tf_op jit(solution)/shard_map/ppermute | solution.py:57
  398.9 21.5 %collective-permute-start.26 = (bf16[2,4,96,768]{3,2,1,0:T(8,128)(2,1)}, bf16[2,4,96,768]{3,2,1,0:T(8,128)(2,1)S(1)}, u32[]{:S(2)}, u32[]{:S(2)}) collective-permute-start(bf16[2,4,96,768]{3,2,1,0:T(8,128)(2,1)} %pad_maximum_fusion.3), channel_id=1, source_target_pairs={{0,16},{1,9},{2,18},{3,11},{4,20},{5,13},{6,22},{7,15},{8,24},{9,1... | collective-permute-start | bytes 3538952 | tf_op jit(solution)/shard_map/ppermute | solution.py:57
  408.3 24.0 %collective-permute-start.20 = (bf16[2,4,24,3072]{3,2,1,0:T(8,128)(2,1)}, bf16[2,4,24,3072]{3,2,1,0:T(8,128)(2,1)S(1)}, u32[]{:S(2)}, u32[]{:S(2)}) collective-permute-start(bf16[2,4,24,3072]{3,2,1,0:T(8,128)(2,1)} %pad_maximum_fusion.2), channel_id=1, source_target_pairs={{0,16},{1,9},{2,18},{3,11},{4,20},{5,13},{6,22},{7,15},{8,24},{9,1... | collective-permute-start | bytes 3538952 | tf_op jit(solution)/shard_map/ppermute | solution.py:57
  421.9 13.9 %collective-permute-start.27 = (bf16[1,4,96,768]{3,2,1,0:T(8,128)(2,1)S(1)}, bf16[1,4,96,768]{3,2,1,0:T(8,128)(2,1)S(1)}, u32[]{:S(2)}, u32[]{:S(2)}) collective-permute-start(bf16[1,4,96,768]{3,2,1,0:T(8,128)(2,1)S(1)} %fusion.23), channel_id=1, source_target_pairs={{0,8},{1,17},{2,10},{3,19},{4,12},{5,21},{6,14},{7,23},{8,0},{9,25... | collective-permute-start | bytes 1769480 | tf_op jit(solution)/shard_map/ppermute | solution.py:57
  437.4 11.8 %collective-permute-start.28 = (bf16[96,768]{1,0:T(8,128)(2,1)S(1)}, bf16[96,768]{1,0:T(8,128)(2,1)S(1)}, u32[]{:S(2)}, u32[]{:S(2)}) collective-permute-start(bf16[96,768]{1,0:T(8,128)(2,1)S(1)} %get-tuple-element.105), channel_id=1, source_target_pairs={{0,2},{1,3},{2,4},{3,5},{4,6},{5,7},{6,0},{7,1},{8,10},{9,11},{10,... | collective-permute-start | bytes 442376 | tf_op jit(solution)/shard_map/ppermute | solution.py:57
  440.0 11.3 %collective-permute-start.30 = (bf16[96,768]{1,0:T(8,128)(2,1)S(1)}, bf16[96,768]{1,0:T(8,128)(2,1)S(1)}, u32[]{:S(2)}, u32[]{:S(2)}) collective-permute-start(bf16[96,768]{1,0:T(8,128)(2,1)S(1)} %get-tuple-element.106), channel_id=1, source_target_pairs={{0,6},{1,7},{2,0},{3,1},{4,2},{5,3},{6,4},{7,5},{8,14},{9,15},{10,... | collective-permute-start | bytes 442376 | tf_op jit(solution)/shard_map/ppermute | solution.py:57
  441.3 19.3 %collective-permute-start.29 = (bf16[96,768]{1,0:T(8,128)(2,1)S(1)}, bf16[96,768]{1,0:T(8,128)(2,1)S(1)}, u32[]{:S(2)}, u32[]{:S(2)}) collective-permute-start(bf16[96,768]{1,0:T(8,128)(2,1)S(1)} %get-tuple-element.107), channel_id=1, source_target_pairs={{0,4},{1,5},{2,6},{3,7},{4,0},{5,1},{6,2},{7,3},{8,12},{9,13},{10,... | collective-permute-start | bytes 442376 | tf_op jit(solution)/shard_map/ppermute | solution.py:57
  445.4 16.0 %collective-permute-start.22 = (bf16[24,3072]{1,0:T(8,128)(2,1)S(1)}, bf16[24,3072]{1,0:T(8,128)(2,1)S(1)}, u32[]{:S(2)}, u32[]{:S(2)}) collective-permute-start(bf16[24,3072]{1,0:T(8,128)(2,1)S(1)} %get-tuple-element.108), channel_id=1, source_target_pairs={{0,2},{1,3},{2,4},{3,5},{4,6},{5,7},{6,0},{7,1},{8,10},{9,11},{10,... | collective-permute-start | bytes 442376 | tf_op jit(solution)/shard_map/ppermute | solution.py:57
  448.2 13.2 %collective-permute-start.24 = (bf16[24,3072]{1,0:T(8,128)(2,1)S(1)}, bf16[24,3072]{1,0:T(8,128)(2,1)S(1)}, u32[]{:S(2)}, u32[]{:S(2)}) collective-permute-start(bf16[24,3072]{1,0:T(8,128)(2,1)S(1)} %get-tuple-element.109), channel_id=1, source_target_pairs={{0,6},{1,7},{2,0},{3,1},{4,2},{5,3},{6,4},{7,5},{8,14},{9,15},{10,... | collective-permute-start | bytes 442376 | tf_op jit(solution)/shard_map/ppermute | solution.py:57
  449.2 15.9 %collective-permute-start.23 = (bf16[24,3072]{1,0:T(8,128)(2,1)S(1)}, bf16[24,3072]{1,0:T(8,128)(2,1)S(1)}, u32[]{:S(2)}, u32[]{:S(2)}) collective-permute-start(bf16[24,3072]{1,0:T(8,128)(2,1)S(1)} %get-tuple-element.110), channel_id=1, source_target_pairs={{0,4},{1,5},{2,6},{3,7},{4,0},{5,1},{6,2},{7,3},{8,12},{9,13},{10,... | collective-permute-start | bytes 442376 | tf_op jit(solution)/shard_map/ppermute | solution.py:57
  (95 other events, 570.0 us)
Sparse Core Ops, SparseCore 0:
  17.3 129.2 all-gather.2
